TPU v7x, 32 devices: a whole 2x2x4 slice. The times are simulated.
32 devices in a mesh: tile: 8 (over z, y), date: 4 (over x, core).
Axes of the slice: x: 2, y: 2, z: 4, core: 2. Of those that a mesh axis runs over, the one named last changes fastest.
Arguments:
- complex_images: bfloat16 [8, 8, 8, 2, 10, 1920], P('date', 'tile')
- segment_position_map: int32 [8, 8], P('tile'), may hold values from 0 to 7, each once within a row
- usable_position_total: int32 [8], P('tile'), may hold values from 4 to 8
- interferogram_epochs: int32 [16, 2], replicated, may hold values from 0 to 7, as said below
Outputs:
- coherence: float32 [16, 2, 16, 1024], P('date', None, None, 'tile')
Inputs may be any that keep to these rules, and one draw needn't show every extreme that they name: Each row of segment_position_map names every block position once. `interferogram_epochs`: the two dates of a pair differ.
All inputs are finite; a program needn't handle non-finite values.
Results may differ from a plain program's by a relative error of at most 0.0003.
Values may be sent and summed in bfloat16 or wider, within the bound.
A program may use at most 128 MiB of HBM per device.

v0:
```python
import jax
import jax.numpy as jnp
from jax import lax
from jax.sharding import PartitionSpec as P

LOOK_RG = 15
LOOK_AZ = 5
EPS = 1e-05


def tile_looks(stack, first_idx, second_idx, valid, box):
    scale = 1.0 / (LOOK_AZ * LOOK_RG)

    def looks(values):
        ranged = jnp.dot(
            values, box, precision=lax.Precision.HIGHEST, preferred_element_type=jnp.float32
        )
        extent = ranged.shape
        return (
            ranged.reshape(extent[:-2] + (extent[-2] // LOOK_AZ, LOOK_AZ, extent[-1])).sum(axis=-2)
            * scale
        )

    def date_power(image):
        image = image.astype(jnp.float32)
        return looks(image[:, 0] * image[:, 0] + image[:, 1] * image[:, 1])

    power = lax.map(date_power, stack)

    def one_pair(indices):
        first = lax.dynamic_index_in_dim(stack, indices[0], 0, keepdims=False).astype(jnp.float32)
        second = lax.dynamic_index_in_dim(stack, indices[1], 0, keepdims=False).astype(jnp.float32)
        cross_re = looks(first[:, 0] * second[:, 0] + first[:, 1] * second[:, 1])
        cross_im = looks(first[:, 1] * second[:, 0] - first[:, 0] * second[:, 1])
        power_first = lax.dynamic_index_in_dim(power, indices[0], 0, keepdims=False)
        power_second = lax.dynamic_index_in_dim(power, indices[1], 0, keepdims=False)
        weight = valid[:, None, None] / jnp.sqrt((power_first + EPS) * (power_second + EPS))
        return jnp.stack([cross_re * weight, cross_im * weight], axis=0)

    return lax.map(one_pair, jnp.stack([first_idx, second_idx], axis=1))


def place_rows(gamma, positions):
    ranking = jnp.argsort(positions)
    placed = jnp.take(gamma, ranking, axis=2)
    extent = placed.shape
    return placed.reshape(extent[0], extent[1], extent[2] * extent[3], extent[4])


def on_device(complex_images, segment_position_map, usable_position_total, interferogram_epochs):
    groups = lax.axis_size("date")
    tile_cols = complex_images.shape[-1]
    box = (
        jnp.arange(tile_cols)[:, None] // LOOK_RG == jnp.arange(tile_cols // LOOK_RG)[None, :]
    ).astype(jnp.float32)
    positions = segment_position_map[0]
    moved = lax.all_to_all(complex_images, "tile", split_axis=2, concat_axis=1, tiled=True)
    stack = moved[:, :, 0]
    valid = (positions < usable_position_total[0]).astype(jnp.float32)
    gathered = lax.all_gather(stack, "date", axis=0, tiled=True)
    mine = interferogram_epochs.shape[0] // groups
    local_pairs = lax.dynamic_slice_in_dim(
        interferogram_epochs, lax.axis_index("date") * mine, mine, 0
    )
    gamma = tile_looks(gathered, local_pairs[:, 0], local_pairs[:, 1], valid, box)
    return place_rows(gamma, positions)


def solution(mesh):
    in_specs = (P("date", "tile", None, None, None, None), P("tile", None), P("tile"), P())
    out_specs = P("date", None, None, "tile")
    return jax.shard_map(
        on_device, mesh=mesh, in_specs=in_specs, out_specs=out_specs, check_vma=False
    )
```

profile of v0, /device:TPU:0, one launch (start us, length us, event | category | flops | bytes accessed | tf_op | source)
XLA Modules:
  0.0 142.8 jit_solution(7151218420765707386)
XLA Ops:
  6.5 2.1 %copy.19 = bf16[2,1,8,2,10,1920]{5,3,4,1,0,2:T(2,128)(2,1)S(1)} copy(bf16[2,1,8,2,10,1920]{5,3,4,2,1,0:T(2,128)(2,1)} %param.8) | data formatting | bytes 2457600 | tf_op args[0]
  8.7 36.9 %all_to_all.4 = bf16[2,1,8,2,10,1920]{5,3,4,1,0,2:T(2,128)(2,1)S(1)} all-to-all(bf16[2,1,8,2,10,1920]{5,3,4,1,0,2:T(2,128)(2,1)S(1)} %copy.19), channel_id=1, replica_groups=mesh['tile'=8,'date'=4] {'tile'}, dimensions={2} | all-to-all | bytes 2457600 | tf_op jit(solution)/shard_map/all_to_all | solution.py:57
  45.6 1.2 copy.20
  47.5 1.0 sort.17
  48.7 35.6 %all-gather.3.cloned.1.call-done = bf16[8,1,8,2,10,1920]{5,2,4,3,1,0:T(8,128)(2,1)} async-done(((bf16[2,1,8,2,10,1920]{5,2,4,3,1,0:T(8,128)(2,1)}), bf16[8,1,8,2,10,1920]{5,2,4,3,1,0:T(8,128)(2,1)}) %all-gather.3.cloned.1.call-update) | async-done | bytes 4915216 | tf_op jit(solution)/shard_map/all_gather | solution.py:60
  84.4 17.9 %while.23 = (s32[]{:T(128)}, f32[8,8,2,128]{3,1,2,0:T(8,128)S(1)}, bf16[8,8,2,10,1920]{4,1,3,2,0:T(8,128)(2,1)}, s32[1920]{0:T(1024)S(1)}, s32[]{:T(128)}) while((s32[]{:T(128)}, f32[8,8,2,128]{3,1,2,0:T(8,128)S(1)}, bf16[8,8,2,10,1920]{4,1,3,2,0:T(8,128)(2,1)}, s32[1920]{0:T(1024)S(1)}, s32[]{:T(128)}) %tuple.60), condition=%wide.region_3.4_spmd.clone, body=%wide.region_1.3_spmd.clone.sunk | while | flops 237199360 | bytes 4333125 | solution.py:28
  84.4 1.2 bitcast_convert_fusion.5
  85.6 1.0 convolution_reduce_fusion.6
  86.6 1.2 bitcast_convert_fusion.5
  87.8 1.0 convolution_reduce_fusion.6
  88.8 1.2 bitcast_convert_fusion.5
  90.1 1.0 convolution_reduce_fusion.6
  91.1 1.2 bitcast_convert_fusion.5
  92.3 1.0 convolution_reduce_fusion.6
  93.3 1.2 bitcast_convert_fusion.5
  94.5 1.0 convolution_reduce_fusion.6
  95.5 1.2 bitcast_convert_fusion.5
  96.8 1.0 convolution_reduce_fusion.6
  97.8 1.2 bitcast_convert_fusion.5
  99.0 1.0 convolution_reduce_fusion.6
  100.0 1.2 bitcast_convert_fusion.5
  101.2 1.0 convolution_reduce_fusion.6
  102.2 32.4 %while.24 = (s32[]{:T(128)}, f32[4,2,8,2,128]{4,0,3,2,1:T(4,128)S(1)}, s32[4,2]{0,1:T(2,128)S(1)}, bf16[8,8,2,10,1920]{4,1,3,2,0:T(8,128)(2,1)}, f32[8]{0:T(128)...) while((s32[]{:T(128)}, ...), condition=%wide.region_7.8_spmd.clone.clone, body=%wide.region_4.7_spmd.clone.clone.sunk | while | flops 474415104 | bytes 8781057 | solution.py:40
  106.6 1.4 bitcast_convert_fusion.6
  108.2 1.0 convolution_reduce_fusion.7
  109.1 1.0 convolution_reduce_fusion.8
  114.7 1.4 bitcast_convert_fusion.6
  116.3 1.0 convolution_reduce_fusion.7
  122.8 1.4 bitcast_convert_fusion.6
  124.4 1.0 convolution_reduce_fusion.7
  130.9 1.4 bitcast_convert_fusion.6
  132.5 1.0 convolution_reduce_fusion.7
  (67 shorter events, 9.1 us)
Async XLA Ops:
  6.5 42.1 %copy-start = (s32[16,2]{0,1:T(2,128)S(1)}, s32[16,2]{0,1:T(2,128)}, u32[]{:S(2)}) copy-start(s32[16,2]{0,1:T(2,128)} %param.11) | copy-start | bytes 388
  6.5 77.8 %all-gather.3.cloned.1.call-start = ((), (), s32[]{:S(2)}) async-start(), calls=%async_computation.1 | async-start | bytes 6144000 | tf_op jit(solution)/shard_map/all_gather | solution.py:60
  46.7 0.7 copy-start.1
Sparse Core Ops, SparseCore 0:
  46.9 37.4 all-gather.2
where the time goes:
time: 144 us; the launch traced here: 143 us
  blocking collectives  36.9 us (26%)
  waiting for transfers between devices  35.6 us (25%)
  other arithmetic  18.1 us (13%)
  matrix products  15.4 us (11%)
  loops' own time  15.3 us (11%)
  between operations  14.1 us (10%)
  local copies, waits for them, and re-layouts  7.39 us (5%)
    all_to_all x1, blocking collectives, on_device(): lax.all_to_all(complex_images, 'tile', split_axis=2, concat_axis=1, tiled...  36.9 us
    all_gather x1, waiting for transfers between devices, on_device(): gathered = lax.all_gather(stack, 'date', axis=0, tiled=True)  35.6 us
    dot_general x16, matrix products, looks(): jnp.dot(values, box, precision=lax.Precision.HIGHEST, preferred_element_t...  15.4 us
    another operation x1, loops' own time, tile_looks(): return lax.map(one_pair, jnp.stack([first_idx, second_idx], axis=1))  15 us
    convert_element_type x8, other arithmetic, date_power(): image = image.astype(jnp.float32)  9.26 us
    convert_element_type x4, other arithmetic, one_pair(): lax.dynamic_index_in_dim(stack, indices[0], 0, keepdims=False)  5.7 us
  transfers between devices with their start and end apart: 1, of which 1 were waited for; matrix products, arithmetic and copies ran while one was open for 1% of the time, Pallas kernels for 0%

commit v1 on v0

--- a/solution.py
+++ b/solution.py
@@ -6,6 +6,23 @@
 LOOK_RG = 15
 LOOK_AZ = 5
 EPS = 1e-05
+
+
+def stops_all_number(local_values):
+    taken_in = lax.axis_size("tile")
+    inter, outer = (taken_in, lax.axis_index("tile"))
+    near = local_values.shape[2] // inter
+    piece_now = list(local_values.shape)
+    piece_now[2] = near
+    long_array = piece_now[1]
+    piece_now[1] = long_array * inter
+    small = jnp.zeros(piece_now, local_values.dtype)
+    for w in [*range(inter)]:
+        main = lax.dynamic_slice_in_dim(local_values, (outer ^ w) * near, near, axis=2)
+        if w:
+            main = lax.ppermute(main, "tile", tuple(((dev_j, dev_j ^ w) for dev_j in range(inter))))
+        small = lax.dynamic_update_slice_in_dim(small, main, (outer ^ w) * long_array, axis=1)
+    return small
 
 
 def tile_looks(stack, first_idx, second_idx, valid, box):
@@ -54,7 +71,7 @@
         jnp.arange(tile_cols)[:, None] // LOOK_RG == jnp.arange(tile_cols // LOOK_RG)[None, :]
     ).astype(jnp.float32)
     positions = segment_position_map[0]
-    moved = lax.all_to_all(complex_images, "tile", split_axis=2, concat_axis=1, tiled=True)
+    moved = stops_all_number(complex_images)
     stack = moved[:, :, 0]
     valid = (positions < usable_position_total[0]).astype(jnp.float32)
     gathered = lax.all_gather(stack, "date", axis=0, tiled=True)

time: 144 us -> 159 us (1.10)
  blocking collectives: 36.9 us -> 0 us
  local copies, waits for them, and re-layouts: 7.39 us -> 28.4 us
  waiting for transfers between devices: 35.6 us -> 52.7 us
  starting transfers between devices: 0.01 us -> 13.4 us
    all_to_all x1 -> x0, blocking collectives: 36.9 us -> none  [on_device(): lax.all_to_all(complex_images, 'tile', split_axis=2, concat_axis=1, tiled...]
    dynamic_update_slice x0 -> x8, local copies, waits for them, and re-layouts: none -> 17.4 us  [stops_all_number(): lax.dynamic_update_slice_in_dim(small, main, (outer ^ w) * long_array, ax...]
    ppermute x0 -> x7, starting transfers between devices: none -> 13.4 us  [stops_all_number(): lax.ppermute(main, 'tile', tuple(((dev_j, dev_j ^ w) for dev_j in range(i...]
    ppermute x0 -> x7, waiting for transfers between devices: none -> 13 us  [stops_all_number(): lax.ppermute(main, 'tile', tuple(((dev_j, dev_j ^ w) for dev_j in range(i...]
    all_gather x1, waiting for transfers between devices: 35.6 us -> 39.7 us  [on_device(): gathered = lax.all_gather(stack, 'date', axis=0, tiled=True)]
    squeeze x0 -> x9, local copies, waits for them, and re-layouts: none -> 3.82 us  [on_device(): stack = moved[:, :, 0]]
    dynamic_slice x0 -> x1, local copies, waits for them, and re-layouts: none -> 2.21 us  [stops_all_number(): lax.dynamic_slice_in_dim(local_values, (outer ^ w) * near, near, axis=2)]
  transfers between devices with their start and end apart: 1 -> 8, of which waited for: 1 -> 3; matrix products, arithmetic and copies ran while one was open for 1% -> 4% of each run, Pallas kernels for 0% -> 0%
where the time goes in v1:
time: 159 us; the launch traced here: 158 us
  waiting for transfers between devices  52.7 us (33%)
  local copies, waits for them, and re-layouts  28.4 us (18%)
  other arithmetic  18.2 us (11%)
  loops' own time  15.4 us (10%)
  matrix products  15.4 us (10%)
  between operations  14.3 us (9%)
  starting transfers between devices  13.4 us (8%)
    all_gather x1, waiting for transfers between devices, on_device(): gathered = lax.all_gather(stack, 'date', axis=0, tiled=True)  39.7 us
    dynamic_update_slice x8, local copies, waits for them, and re-layouts, stops_all_number(): lax.dynamic_update_slice_in_dim(small, main, (outer ^ w) * long_array, ax...  17.4 us
    dot_general x16, matrix products, looks(): jnp.dot(values, box, precision=lax.Precision.HIGHEST, preferred_element_t...  15.4 us
    another operation x1, loops' own time, tile_looks(): return lax.map(one_pair, jnp.stack([first_idx, second_idx], axis=1))  15.1 us
    ppermute x7, starting transfers between devices, stops_all_number(): lax.ppermute(main, 'tile', tuple(((dev_j, dev_j ^ w) for dev_j in range(i...  13.4 us
    ppermute x7, waiting for transfers between devices, stops_all_number(): lax.ppermute(main, 'tile', tuple(((dev_j, dev_j ^ w) for dev_j in range(i...  13 us
    convert_element_type x8, other arithmetic, date_power(): image = image.astype(jnp.float32)  9.26 us
    convert_element_type x4, other arithmetic, one_pair(): lax.dynamic_index_in_dim(stack, indices[0], 0, keepdims=False)  5.7 us
  transfers between devices with their start and end apart: 8, of which 3 were waited for; matrix products, arithmetic and copies ran while one was open for 4% of the time, Pallas kernels for 0%

profile of v1, /device:TPU:0, one launch (start us, length us, event | category | flops | bytes accessed | tf_op | source)
XLA Modules:
  0.0 157.7 jit_solution(13649408793435155503)
XLA Ops:
  6.5 2.2 %constant_dynamic-slice_fusion.1 = (bf16[2,1,1,2,10,1920]{5,3,4,2,1,0:T(2,128)(2,1)S(1)}, bf16[2,1,1,2,10,1920]{5,3,4,2,1,0:T(2,128)(2,1)S(1)}, bf16[2,1,1,2,10,...) fusion(bf16[2,1,8,2,10,1920]{5,3,4,2,1,0:T(2,128)(2,1)} %param., ...), kind=kLoop, calls=%fused_computation.42 | loop fusion | bytes 2457632 | tf_op jit(solution)/shard_map/dynamic_slice | solution.py:21
  8.8 3.1 %collective-permute-start = (bf16[2,1,1,2,10,1920]{5,3,4,2,1,0:T(2,128)(2,1)S(1)}, bf16[2,1,1,2,10,1920]{5,3,4,2,1,0:T(2,128)(2,1)S(1)}, u32[]{:S(2)}, u32[]{:S(2)}) collective-permute-start(bf16[2,1,1,2,10,1920]{5,3,4,2,1,0:T(2,128)(2,1)S(1)} %get-tuple-element.152), channel_id=1, source_target_pairs={{0,4},{4,0},{8,12},{12,8},{16,20},{20,16},{24,28},{28,24},{1,5},{5... | collective-permute-start | bytes 460808 | tf_op jit(solution)/shard_map/ppermute | solution.py:23
  11.8 1.6 collective-permute-start.1
  13.4 3.0 %collective-permute-start.3 = (bf16[2,1,1,2,10,1920]{5,3,4,2,1,0:T(2,128)(2,1)S(1)}, bf16[2,1,1,2,10,1920]{5,3,4,2,1,0:T(2,128)(2,1)S(1)}, u32[]{:S(2)}, u32[]{:S(2)}) collective-permute-start(bf16[2,1,1,2,10,1920]{5,3,4,2,1,0:T(2,128)(2,1)S(1)} %get-tuple-element.149), channel_id=1, source_target_pairs={{0,16},{4,20},{8,24},{12,28},{16,0},{20,4},{24,8},{28,12},{1,17},{... | collective-permute-start | bytes 460808 | tf_op jit(solution)/shard_map/ppermute | solution.py:23
  16.4 1.3 collective-permute-start.4
  17.7 3.6 %collective-permute-start.5 = (bf16[2,1,1,2,10,1920]{5,3,4,2,1,0:T(2,128)(2,1)S(1)}, bf16[2,1,1,2,10,1920]{5,3,4,2,1,0:T(2,128)(2,1)}, u32[]{:S(2)}, u32[]{:S(2)}) collective-permute-start(bf16[2,1,1,2,10,1920]{5,3,4,2,1,0:T(2,128)(2,1)S(1)} %get-tuple-element.154), channel_id=1, source_target_pairs={{0,24},{4,28},{8,16},{12,20},{16,8},{20,12},{24,0},{28,4},{1,25},{... | collective-permute-start | bytes 460808 | tf_op jit(solution)/shard_map/ppermute | solution.py:23
  21.3 2.9 %collective-permute-done.1 = bf16[2,1,1,2,10,1920]{5,3,4,2,1,0:T(2,128)(2,1)S(1)} collective-permute-done((bf16[2,1,1,2,10,1920]{5,3,4,2,1,0:T(2,128)(2,1)S(1)}, bf16[2,1,1,2,10,1920]{5,3,4,2,1,0:T(2,128)(2,1)S(1)}, u32[]{:S(2)}, u32[]{:S(2)}) %collective-permute-start.1) | collective-permute-done | bytes 153632 | tf_op jit(solution)/shard_map/ppermute | solution.py:23
  25.5 2.2 %dynamic_update_slice.40 = bf16[2,8,2,10,1920]{4,1,3,2,0:T(8,128)(2,1)S(1)} dynamic-update-slice(bf16[2,8,2,10,1920]{4,1,3,2,0:T(8,128)(2,1)S(1)} %squeeze.56, bf16[2,1,2,10,1920]{4,1,3,2,0:T(2,128)(2,1)S(1)} %copy.41, s32[]{:T(128)} %constant.87.clone.1, s32[]{:T(128)S(6)} %select_n.71, s32[]{:T(128)} %constant.87.clone.1, s32[]{:T(128)} %constant.87.clone.1, s32[]{:T(128)} %constant.87.clone.1) | dynamic-update-slice | bytes 307204 | tf_op jit(solution)/shard_map/dynamic_update_slice | solution.py:24
  28.6 10.0 %collective-permute-done.4 = bf16[2,1,1,2,10,1920]{5,3,4,2,1,0:T(2,128)(2,1)S(1)} collective-permute-done((bf16[2,1,1,2,10,1920]{5,3,4,2,1,0:T(2,128)(2,1)S(1)}, bf16[2,1,1,2,10,1920]{5,3,4,2,1,0:T(2,128)(2,1)S(1)}, u32[]{:S(2)}, u32[]{:S(2)}) %collective-permute-start.4) | collective-permute-done | bytes 153632 | tf_op jit(solution)/shard_map/ppermute | solution.py:23
  40.1 1.2 copy.48
  41.2 2.2 %dynamic_update_slice.41 = bf16[2,8,2,10,1920]{4,1,3,2,0:T(8,128)(2,1)S(1)} dynamic-update-slice(bf16[2,8,2,10,1920]{4,1,3,2,0:T(8,128)(2,1)S(1)} %dynamic_update_slice.40, bf16[2,1,2,10,1920]{4,1,3,2,0:T(2,128)(2,1)S(1)} %copy.42, s32[]{:T(128)} %constant.87.clone.1, s32[]{:T(128)S(6)} %select_n.72, s32[]{:T(128)} %constant.87.clone.1, s32[]{:T(128)} %constant.87.clone.1, s32[]{:T(128)} %constant.87.clone.1) | dynamic-update-slice | bytes 307204 | tf_op jit(solution)/shard_map/dynamic_update_slice | solution.py:24
  43.4 2.2 %dynamic_update_slice.42 = bf16[2,8,2,10,1920]{4,1,3,2,0:T(8,128)(2,1)S(1)} dynamic-update-slice(bf16[2,8,2,10,1920]{4,1,3,2,0:T(8,128)(2,1)S(1)} %dynamic_update_slice.41, bf16[2,1,2,10,1920]{4,1,3,2,0:T(2,128)(2,1)S(1)} %copy.43, s32[]{:T(128)} %constant.87.clone.1, s32[]{:T(128)S(6)} %select_n.73, s32[]{:T(128)} %constant.87.clone.1, s32[]{:T(128)} %constant.87.clone.1, s32[]{:T(128)} %constant.87.clone.1) | dynamic-update-slice | bytes 307204 | tf_op jit(solution)/shard_map/dynamic_update_slice | solution.py:24
  45.6 2.2 %dynamic_update_slice.43 = bf16[2,8,2,10,1920]{4,1,3,2,0:T(8,128)(2,1)S(1)} dynamic-update-slice(bf16[2,8,2,10,1920]{4,1,3,2,0:T(8,128)(2,1)S(1)} %dynamic_update_slice.42, bf16[2,1,2,10,1920]{4,1,3,2,0:T(2,128)(2,1)S(1)} %copy.44, s32[]{:T(128)} %constant.87.clone.1, s32[]{:T(128)S(6)} %select_n.74, s32[]{:T(128)} %constant.87.clone.1, s32[]{:T(128)} %constant.87.clone.1, s32[]{:T(128)} %constant.87.clone.1) | dynamic-update-slice | bytes 307204 | tf_op jit(solution)/shard_map/dynamic_update_slice | solution.py:24
  47.8 2.2 %dynamic_update_slice.44 = bf16[2,8,2,10,1920]{4,1,3,2,0:T(8,128)(2,1)S(1)} dynamic-update-slice(bf16[2,8,2,10,1920]{4,1,3,2,0:T(8,128)(2,1)S(1)} %dynamic_update_slice.43, bf16[2,1,2,10,1920]{4,1,3,2,0:T(2,128)(2,1)S(1)} %copy.45, s32[]{:T(128)} %constant.87.clone.1, s32[]{:T(128)S(6)} %select_n.75, s32[]{:T(128)} %constant.87.clone.1, s32[]{:T(128)} %constant.87.clone.1, s32[]{:T(128)} %constant.87.clone.1) | dynamic-update-slice | bytes 307204 | tf_op jit(solution)/shard_map/dynamic_update_slice | solution.py:24
  50.0 2.2 %dynamic_update_slice.45 = bf16[2,8,2,10,1920]{4,1,3,2,0:T(8,128)(2,1)S(1)} dynamic-update-slice(bf16[2,8,2,10,1920]{4,1,3,2,0:T(8,128)(2,1)S(1)} %dynamic_update_slice.44, bf16[2,1,2,10,1920]{4,1,3,2,0:T(2,128)(2,1)S(1)} %copy.46, s32[]{:T(128)} %constant.87.clone.1, s32[]{:T(128)S(6)} %select_n.76, s32[]{:T(128)} %constant.87.clone.1, s32[]{:T(128)} %constant.87.clone.1, s32[]{:T(128)} %constant.87.clone.1) | dynamic-update-slice | bytes 307204 | tf_op jit(solution)/shard_map/dynamic_update_slice | solution.py:24
  52.2 2.2 %dynamic_update_slice.46 = bf16[2,8,2,10,1920]{4,1,3,2,0:T(8,128)(2,1)S(1)} dynamic-update-slice(bf16[2,8,2,10,1920]{4,1,3,2,0:T(8,128)(2,1)S(1)} %dynamic_update_slice.45, bf16[2,1,2,10,1920]{4,1,3,2,0:T(2,128)(2,1)S(1)} %copy.47, s32[]{:T(128)} %constant.87.clone.1, s32[]{:T(128)S(6)} %select_n.77, s32[]{:T(128)} %constant.87.clone.1, s32[]{:T(128)} %constant.87.clone.1, s32[]{:T(128)} %constant.87.clone.1) | dynamic-update-slice | bytes 307204 | tf_op jit(solution)/shard_map/dynamic_update_slice | solution.py:24
  54.4 2.2 %dynamic_update_slice.47 = bf16[2,8,2,10,1920]{4,1,3,2,0:T(8,128)(2,1)S(1)} dynamic-update-slice(bf16[2,8,2,10,1920]{4,1,3,2,0:T(8,128)(2,1)S(1)} %dynamic_update_slice.46, bf16[2,1,2,10,1920]{4,1,3,2,0:T(2,128)(2,1)S(1)} %copy.48, s32[]{:T(128)} %constant.87.clone.1, s32[]{:T(128)S(6)} %select_n.78, s32[]{:T(128)} %constant.87.clone.1, s32[]{:T(128)} %constant.87.clone.1, s32[]{:T(128)} %constant.87.clone.1) | dynamic-update-slice | bytes 307204 | tf_op jit(solution)/shard_map/dynamic_update_slice | solution.py:24
  59.6 39.7 %all-gather.2.cloned.1.call-done = bf16[8,8,2,10,1920]{4,1,3,2,0:T(8,128)(2,1)} async-done(((bf16[2,8,2,10,1920]{4,1,3,2,0:T(8,128)(2,1)}), bf16[8,8,2,10,1920]{4,1,3,2,0:T(8,128)(2,1)}) %all-gather.2.cloned.1.call-update) | async-done | bytes 4915216 | tf_op jit(solution)/shard_map/all_gather | solution.py:77
  99.3 17.9 %while.23 = (s32[]{:T(128)}, f32[8,8,2,128]{3,1,2,0:T(8,128)S(1)}, bf16[8,8,2,10,1920]{4,1,3,2,0:T(8,128)(2,1)}, s32[1920]{0:T(1024)S(1)}, s32[]{:T(128)}) while((s32[]{:T(128)}, f32[8,8,2,128]{3,1,2,0:T(8,128)S(1)}, bf16[8,8,2,10,1920]{4,1,3,2,0:T(8,128)(2,1)}, s32[1920]{0:T(1024)S(1)}, s32[]{:T(128)}) %tuple.59), condition=%wide.region_3.4_spmd.clone, body=%wide.region_1.3_spmd.clone.sunk | while | flops 237199360 | bytes 4333125 | solution.py:45
  99.3 1.2 bitcast_convert_fusion.5
  101.6 1.2 bitcast_convert_fusion.5
  103.8 1.2 bitcast_convert_fusion.5
  106.0 1.2 bitcast_convert_fusion.5
  108.3 1.2 bitcast_convert_fusion.5
  110.5 1.2 bitcast_convert_fusion.5
  112.7 1.2 bitcast_convert_fusion.5
  115.0 1.2 bitcast_convert_fusion.5
  117.2 32.4 %while.24 = (s32[]{:T(128)}, f32[4,2,8,2,128]{4,0,3,2,1:T(4,128)S(1)}, s32[4,2]{0,1:T(2,128)S(1)}, bf16[8,8,2,10,1920]{4,1,3,2,0:T(8,128)(2,1)}, f32[8]{0:T(128)...) while((s32[]{:T(128)}, ...), condition=%wide.region_7.8_spmd.clone.clone, body=%wide.region_4.7_spmd.clone.clone.sunk | while | flops 474415104 | bytes 8781057 | solution.py:57
  121.6 1.4 bitcast_convert_fusion.6
  129.7 1.4 bitcast_convert_fusion.6
  137.7 1.4 bitcast_convert_fusion.6
  145.8 1.4 bitcast_convert_fusion.6
  (98 shorter events, 27.2 us)
Async XLA Ops:
  6.5 53.0 %copy-start = (s32[16,2]{0,1:T(2,128)S(1)}, s32[16,2]{0,1:T(2,128)}, u32[]{:S(2)}) copy-start(s32[16,2]{0,1:T(2,128)} %param.11) | copy-start | bytes 388
  6.5 92.8 %all-gather.2.cloned.1.call-start = ((), (), s32[]{:S(2)}) async-start(), calls=%async_computation | async-start | bytes 6144000 | tf_op jit(solution)/shard_map/all_gather | solution.py:77
  8.8 8.9 %collective-permute-start = (bf16[2,1,1,2,10,1920]{5,3,4,2,1,0:T(2,128)(2,1)S(1)}, bf16[2,1,1,2,10,1920]{5,3,4,2,1,0:T(2,128)(2,1)S(1)}, u32[]{:S(2)}, u32[]{:S(2)}) collective-permute-start(bf16[2,1,1,2,10,1920]{5,3,4,2,1,0:T(2,128)(2,1)S(1)} %get-tuple-element.152), channel_id=1, source_target_pairs={{0,4},{4,0},{8,12},{12,8},{16,20},{20,16},{24,28},{28,24},{1,5},{5... | collective-permute-start | bytes 460808 | tf_op jit(solution)/shard_map/ppermute | solution.py:23
  11.8 12.4 %collective-permute-start.1 = (bf16[2,1,1,2,10,1920]{5,3,4,2,1,0:T(2,128)(2,1)S(1)}, bf16[2,1,1,2,10,1920]{5,3,4,2,1,0:T(2,128)(2,1)S(1)}, u32[]{:S(2)}, u32[]{:S(2)}) collective-permute-start(bf16[2,1,1,2,10,1920]{5,3,4,2,1,0:T(2,128)(2,1)S(1)} %get-tuple-element.151), channel_id=1, source_target_pairs={{0,8},{4,12},{8,0},{12,4},{16,24},{20,28},{24,16},{28,20},{1,9},{5... | collective-permute-start | bytes 460808 | tf_op jit(solution)/shard_map/ppermute | solution.py:23
  13.4 14.7 %collective-permute-start.2 = (bf16[2,1,1,2,10,1920]{5,3,4,2,1,0:T(2,128)(2,1)S(1)}, bf16[2,1,1,2,10,1920]{5,3,4,2,1,0:T(2,128)(2,1)S(1)}, u32[]{:S(2)}, u32[]{:S(2)}) collective-permute-start(bf16[2,1,1,2,10,1920]{5,3,4,2,1,0:T(2,128)(2,1)S(1)} %get-tuple-element.150), channel_id=1, source_target_pairs={{0,12},{4,8},{8,4},{12,0},{16,28},{20,24},{24,20},{28,16},{1,13},{... | collective-permute-start | bytes 460808 | tf_op jit(solution)/shard_map/ppermute | solution.py:23
  13.4 15.0 %collective-permute-start.3 = (bf16[2,1,1,2,10,1920]{5,3,4,2,1,0:T(2,128)(2,1)S(1)}, bf16[2,1,1,2,10,1920]{5,3,4,2,1,0:T(2,128)(2,1)S(1)}, u32[]{:S(2)}, u32[]{:S(2)}) collective-permute-start(bf16[2,1,1,2,10,1920]{5,3,4,2,1,0:T(2,128)(2,1)S(1)} %get-tuple-element.149), channel_id=1, source_target_pairs={{0,16},{4,20},{8,24},{12,28},{16,0},{20,4},{24,8},{28,12},{1,17},{... | collective-permute-start | bytes 460808 | tf_op jit(solution)/shard_map/ppermute | solution.py:23
  16.4 22.3 %collective-permute-start.4 = (bf16[2,1,1,2,10,1920]{5,3,4,2,1,0:T(2,128)(2,1)S(1)}, bf16[2,1,1,2,10,1920]{5,3,4,2,1,0:T(2,128)(2,1)S(1)}, u32[]{:S(2)}, u32[]{:S(2)}) collective-permute-start(bf16[2,1,1,2,10,1920]{5,3,4,2,1,0:T(2,128)(2,1)S(1)} %get-tuple-element.148), channel_id=1, source_target_pairs={{0,20},{4,16},{8,28},{12,24},{16,4},{20,0},{24,12},{28,8},{1,21},{... | collective-permute-start | bytes 460808 | tf_op jit(solution)/shard_map/ppermute | solution.py:23
  17.7 21.2 %collective-permute-start.5 = (bf16[2,1,1,2,10,1920]{5,3,4,2,1,0:T(2,128)(2,1)S(1)}, bf16[2,1,1,2,10,1920]{5,3,4,2,1,0:T(2,128)(2,1)}, u32[]{:S(2)}, u32[]{:S(2)}) collective-permute-start(bf16[2,1,1,2,10,1920]{5,3,4,2,1,0:T(2,128)(2,1)S(1)} %get-tuple-element.154), channel_id=1, source_target_pairs={{0,24},{4,28},{8,16},{12,20},{16,8},{20,12},{24,0},{28,4},{1,25},{... | collective-permute-start | bytes 460808 | tf_op jit(solution)/shard_map/ppermute | solution.py:23
  24.2 15.9 %collective-permute-start.6 = (bf16[2,1,1,2,10,1920]{5,3,4,2,1,0:T(2,128)(2,1)S(1)}, bf16[2,1,1,2,10,1920]{5,3,4,2,1,0:T(2,128)(2,1)}, u32[]{:S(2)}, u32[]{:S(2)}) collective-permute-start(bf16[2,1,1,2,10,1920]{5,3,4,2,1,0:T(2,128)(2,1)S(1)} %get-tuple-element.147), channel_id=1, source_target_pairs={{0,28},{4,24},{8,20},{12,16},{16,12},{20,8},{24,4},{28,0},{1,29},{... | collective-permute-start | bytes 460808 | tf_op jit(solution)/shard_map/ppermute | solution.py:23
  52.2 6.1 %copy-start.2 = (s32[1,8]{1,0:T(1,128)S(1)}, s32[1,8]{1,0:T(1,128)}, u32[]{:S(2)}) copy-start(s32[1,8]{1,0:T(1,128)} %param.9) | copy-start | bytes 100
  56.5 1.1 copy-start.1
Sparse Core Ops, SparseCore 0:
  57.7 41.5 all-gather.1
